TPU v7x, 256 devices: a whole 4x4x8 slice. The times are simulated.
256 devices in a mesh: sym: 8 (over y, core), rows: 32 (over z, x).
Axes of the slice: x: 4, y: 4, z: 8, core: 2. Of those that a mesh axis runs over, the one named last changes fastest.
Arguments:
- coeffs: bfloat16 [16384, 8192], P('rows', 'sym'), may hold values from -6 to 6
- beta_op: bfloat16 [8, 1024, 1024], P('sym'), may hold values from -0.1875 to 0.1875
- mix_op: bfloat16 [8, 8, 8, 128, 128], P('sym'), may hold values from -0.125 to 0.125
- pair_op: bfloat16 [8, 128, 128], replicated, may hold values from -0.1875 to 0.1875
- send_list: int32 [32, 32, 2], replicated, may hold values from -1 to 3, as said below
- mix_slot: int32 [128, 16], replicated, may hold values from 0 to 63, as said below
- mix_sign: int32 [128, 16], replicated, may hold values from 0 to 1
- mix_pair: int32 [128, 16], replicated, may hold values from 0 to 7
- aa_src: int32 [128, 8], replicated, may hold values from 0 to 127
- aa_sign: int32 [128, 8], replicated, may hold values from 0 to 1
- aa_pair: int32 [128, 8], replicated, may hold values from 0 to 7
Outputs:
- sigma: float32 [16384, 8192], P('rows', 'sym')
Inputs may be any that keep to these rules, and one draw needn't show every extreme that they name: send_list[s, r, c] is the block, counted within device s's own 4 alpha blocks, that s sends to device r in slot c, or -1 for an empty slot; live slots of a pair come first and hold distinct blocks; every device sends at least one block to itself; in every draw some device receives 2 blocks from every device. mix_slot[P, l] = s * 2 + c names slot c of send_list[s, P // 4], always a live one; every live slot sent to a device is named by some entry of that device's destination blocks.
All inputs are finite; a program needn't handle non-finite values.
Results may differ from a plain program's by a relative error of at most 0.0075.
Values may be sent and summed in bfloat16 or wider, within the bound.
No kernel may reach another device: no remote copies, remote signals or barrier semaphores. Data moves between devices by JAX's collectives and lax.ppermute only.
A program may use at most 128 MiB of HBM per device.

v0:
```python
import jax
import jax.numpy as jnp
from jax import lax
from jax.sharding import PartitionSpec as P

TILE = 128
BT = 8
ABLK = 4
CAP = 2
NPA = 8


def cut_along(array, dim, devices):
    dims = array.shape
    parts = array.reshape(*dims[:dim], devices, dims[dim] // devices, *dims[dim + 1 :])
    return jnp.moveaxis(parts, dim, 0)


def piece_ends(length, count):
    hop = length // count
    if hop >= 8:
        hop -= hop % 8
    return [hop * k for k in range(1, count)]


def laid_out(parts, dim):
    dims = list(parts.shape[1:])
    dims[dim] *= parts.shape[0]
    return jnp.moveaxis(parts, 0, dim).reshape(dims)


def exchange_in_pieces(array, axis, pieces, split_dim, concat_dim):
    parts = cut_along(array, split_dim, lax.axis_size(axis))
    widest = max(range(1, max(2, parts.ndim - 1)), key=lambda d: parts.shape[d])
    finished = []
    for slab in jnp.split(parts, piece_ends(parts.shape[widest], pieces), axis=widest):
        if slab.size:
            finished.append(lax.all_to_all(slab, axis, split_axis=0, concat_axis=0, tiled=True))
    return laid_out(jnp.concatenate(finished, axis=widest), concat_dim)


def per_device(
    coeffs,
    beta_op,
    mix_op,
    pair_op,
    send_list,
    mix_slot,
    mix_sign,
    mix_pair,
    aa_src,
    aa_sign,
    aa_pair,
):
    rows_here, beta_here = coeffs.shape
    sectors = lax.axis_size("sym")
    rank_count = lax.axis_size("rows")
    sector = lax.axis_index("sym")
    block_count = aa_src.shape[0]
    total_rows = block_count * TILE
    col_width = beta_here // rank_count
    local_term = jnp.dot(coeffs, beta_op[0], preferred_element_type=jnp.float32)
    flipped = coeffs.T
    columns = lax.all_to_all(flipped, "rows", split_axis=0, concat_axis=1, tiled=True)
    col_blocks = columns.reshape(col_width, block_count, TILE)
    picked = jnp.take(col_blocks, aa_src, axis=1)
    operator_ids = jnp.arange(NPA, dtype=jnp.int32)
    aa_weight = (
        (1 - 2 * aa_sign)[:, :, None]
        * (aa_pair[:, :, None] == operator_ids[None, None, :]).astype(jnp.int32)
    ).astype(jnp.bfloat16)
    combined = jnp.einsum(
        "cpki,pkg->cpgi", picked, aa_weight, preferred_element_type=jnp.float32
    ).astype(jnp.bfloat16)
    alpha_part = jnp.einsum(
        "cpgj,gij->cpi", combined, pair_op, preferred_element_type=jnp.float32
    ).reshape(col_width, total_rows)
    returned = lax.all_to_all(
        alpha_part.astype(jnp.bfloat16), "rows", split_axis=1, concat_axis=0, tiled=True
    ).astype(alpha_part.dtype)
    dest_ids = jnp.arange(sectors, dtype=jnp.int32)
    pair_of = jnp.bitwise_xor(sector, dest_ids)
    operators = jnp.take(mix_op[0], pair_of, axis=0)
    sign_all = (1 - 2 * mix_sign).astype(jnp.float32)
    slot_src = mix_slot // CAP
    slot_pos = mix_slot % CAP
    dest_rank = (jnp.arange(block_count, dtype=jnp.int32) // ABLK)[:, None]
    owned_blk = send_list[slot_src, dest_rank, slot_pos]
    source = slot_src * ABLK + owned_blk
    gathered = jnp.take(col_blocks, source, axis=1)
    mix_weight = (
        sign_all[None, :, :] * (mix_pair[None, :, :] == pair_of[:, None, None]).astype(jnp.float32)
    ).astype(jnp.bfloat16)
    combos = jnp.einsum(
        "cpli,dpl->dcpi", gathered, mix_weight, preferred_element_type=jnp.float32
    ).astype(jnp.bfloat16)
    combos = combos.reshape(sectors, col_width, total_rows)
    came_back = exchange_in_pieces(combos, "rows", 2, 2, 1)
    inputs = came_back.reshape(sectors, BT, TILE, rows_here)
    contract_eq = "dtkr,dtkj->drtj"
    row_count = lax.axis_size("sym") * rows_here
    products = jnp.einsum(contract_eq, inputs, operators, preferred_element_type=jnp.float32)
    mixed = lax.psum_scatter(
        products.reshape(row_count, beta_here).astype(jnp.bfloat16),
        "sym",
        scatter_dimension=0,
        tiled=True,
    ).astype(jnp.float32)
    return local_term + returned.T + mixed


def solution(mesh):
    in_specs = (
        P("rows", "sym"),
        P("sym", None, None),
        P("sym", None, None, None, None),
        P(),
        P(),
        P(),
        P(),
        P(),
        P(),
        P(),
        P(),
    )
    out_specs = P("rows", "sym")
    return jax.shard_map(
        per_device, mesh=mesh, in_specs=in_specs, out_specs=out_specs, check_vma=False
    )
```

profile of v0, /device:TPU:18, one launch (start us, length us, event | category | flops | bytes accessed | tf_op | source)
XLA Modules:
  0.0 472.6 jit_solution(12893267071110367578)
XLA Ops:
  6.5 2.4 copy.74
  9.0 11.6 %all-to-all-start = ((bf16[32,32,512]{2,1,0:T(8,128)(2,1)}), bf16[32,32,512]{2,1,0:T(8,128)(2,1)S(1)}, u32[]{:S(2)}, u32[]{:S(2)}) async-start(bf16[32,32,512]{2,1,0:T(8,128)(2,1)} %bitcast.84), calls=%async_computation | async-start | bytes 2097152 | tf_op jit(solution)/shard_map/all_to_all | solution.py:64
  21.5 20.1 %gather_fusion.2 = s32[2048]{0:T(1024)S(1)} fusion(s32[32,32,2]{1,2,0:T(2,128)S(1)} %copy-done.1, s32[2048]{0:T(1024)S(1)} %reshape.96), kind=kCustom, calls=%fused_computation.2 | custom fusion | bytes 40960 | tf_op jit(solution)/shard_map/gather | solution.py:88
  42.4 6.2 %all-to-all-done = bf16[32,32,512]{2,1,0:T(8,128)(2,1)S(1)} async-done(((bf16[32,32,512]{2,1,0:T(8,128)(2,1)}), bf16[32,32,512]{2,1,0:T(8,128)(2,1)S(1)}, u32[]{:S(2)}, u32[]{:S(2)}) %all-to-all-start) | async-done | bytes 1048608 | tf_op jit(solution)/shard_map/all_to_all | solution.py:64
  50.2 2.5 reshape.78
  52.7 1.9 copy.77
  54.6 19.2 %gather_fusion.3 = bf16[2048,32,128]{2,1,0:T(8,128)(2,1)} fusion(bf16[32,128,128]{2,0,1:T(8,128)(2,1)S(1)} %copy.77, s32[2048]{0:T(1024)S(1)} %broadcast_clamp_fusion), kind=kCustom, calls=%fused_computation.3 | custom fusion | bytes 33562624 | tf_op jit(solution)/shard_map/jit(_take)/gather | solution.py:90
  73.8 14.4 %select_bitcast_fusion = bf16[32,128,16,128]{3,0,2,1:T(8,128)(2,1)} fusion(bf16[128,16,32,128]{3,2,1,0:T(8,128)(2,1)} %bitcast.76, pred[128,16]{1,0:T(8,128)(4,1)S(1)} %copy.86), kind=kLoop, calls=%fused_computation.6 | loop fusion | flops 8388608 | bytes 33556480 | tf_op jit(solution)/shard_map/jit(_take)/select_n | solution.py:90
  88.2 25.9 %convert_bitcast_fusion.1 = bf16[8,32,128,128]{3,0,1,2:T(8,128)(2,1)} fusion(bf16[32,128,16,128]{3,0,2,1:T(8,128)(2,1)} %select_bitcast_fusion, bf16[128,16]{1,0:T(8,128)(2,1)S(1)} %copy.83, s32[128,16]{1,0:T(8,128)S(1)} %copy.82, s32[8]{0:T(128)S(1)} %iota_xor_fusion), kind=kOutput, calls=%fused_computation.15 | convolution fusion | flops 138444800 | bytes 25178144 | tf_op jit(solution)/shard_map/cpli,dpl->dcpi/dot_general | solution.py:94
  114.1 12.0 %copy.90 = bf16[8,32,128,128]{3,2,1,0:T(8,128)(2,1)} copy(bf16[8,32,128,128]{3,0,1,2:T(8,128)(2,1)} %convert_bitcast_fusion.1) | data formatting | bytes 16777216 | tf_op jit(solution)/shard_map/convert_element_type | solution.py:96
  126.1 14.0 %reshape_reshape.6 = bf16[8,32,32,512]{3,2,1,0:T(8,128)(2,1)} reshape(bf16[8,32,128,128]{3,2,1,0:T(8,128)(2,1)} %copy.90) | data formatting | bytes 16777216 | tf_op jit(solution)/shard_map/reshape;reshape | solution.py:15
  140.1 5.3 %fusion.51 = (bf16[32,8,16,512]{3,0,2,1:T(8,128)(2,1)S(1)}, bf16[32,8,16,512]{3,0,2,1:T(8,128)(2,1)}) fusion(bf16[32,8,32,512]{3,0,2,1:T(8,128)(2,1)} %bitcast.79), kind=kLoop, calls=%fused_computation.83 | loop fusion | bytes 16777216 | tf_op jit(solution)/shard_map/split | solution.py:36
  145.4 4.3 copy.91
  149.7 5.6 %all-to-all-start.2 = ((bf16[32,8,16,512]{3,2,1,0:T(8,128)(2,1)}), bf16[32,8,16,512]{3,2,1,0:T(8,128)(2,1)}, u32[]{:S(2)}, u32[]{:S(2)}) async-start(bf16[32,8,16,512]{3,2,1,0:T(8,128)(2,1)} %copy.91), calls=%async_computation.2 | async-start | bytes 8388608 | tf_op jit(solution)/shard_map/all_to_all | solution.py:38
  155.3 6.5 %copy.92 = bf16[32,8,16,512]{3,2,1,0:T(8,128)(2,1)} copy(bf16[32,8,16,512]{3,0,2,1:T(8,128)(2,1)} %get-tuple-element.8) | data formatting | bytes 8388608 | tf_op jit(solution)/shard_map/split | solution.py:36
  161.8 85.3 %all-to-all-done.2 = bf16[32,8,16,512]{3,2,1,0:T(8,128)(2,1)} async-done(((bf16[32,8,16,512]{3,2,1,0:T(8,128)(2,1)}), bf16[32,8,16,512]{3,2,1,0:T(8,128)(2,1)}, u32[]{:S(2)}, u32[]{:S(2)}) %all-to-all-start.2) | async-done | bytes 4194336 | tf_op jit(solution)/shard_map/all_to_all | solution.py:38
  247.2 8.4 %all-to-all-start.3 = ((bf16[32,8,16,512]{3,2,1,0:T(8,128)(2,1)}), bf16[32,8,16,512]{3,2,1,0:T(8,128)(2,1)}, u32[]{:S(2)}, u32[]{:S(2)}) async-start(bf16[32,8,16,512]{3,2,1,0:T(8,128)(2,1)} %copy.92), calls=%async_computation.3 | async-start | bytes 8388608 | tf_op jit(solution)/shard_map/all_to_all | solution.py:38
  255.7 2.1 gather_fusion.1
  257.8 90.0 %all-to-all-done.3 = bf16[32,8,16,512]{3,2,1,0:T(8,128)(2,1)} async-done(((bf16[32,8,16,512]{3,2,1,0:T(8,128)(2,1)}), bf16[32,8,16,512]{3,2,1,0:T(8,128)(2,1)}, u32[]{:S(2)}, u32[]{:S(2)}) %all-to-all-start.3) | async-done | bytes 4194336 | tf_op jit(solution)/shard_map/all_to_all | solution.py:38
  347.8 8.2 %maximum_bitcast_fusion = bf16[8,32,32,512]{3,2,0,1:T(8,128)(2,1)} fusion(bf16[32,8,16,512]{3,2,1,0:T(8,128)(2,1)} %all-to-all-done.3, bf16[32,8,16,512]{3,2,1,0:T(8,128)(2,1)} %all-to-all-done.2), kind=kLoop, calls=%fused_computation.8 | loop fusion | flops 16777216 | bytes 16777216 | tf_op jit(solution)/shard_map/transpose | solution.py:29
  356.0 8.4 %copy.93 = bf16[8,32,32,512]{3,2,1,0:T(8,128)(2,1)} copy(bf16[8,32,32,512]{3,2,0,1:T(8,128)(2,1)} %maximum_bitcast_fusion) | data formatting | bytes 16777216 | tf_op jit(solution)/shard_map/transpose | solution.py:29
  364.5 9.1 %convert_bitcast_fusion = bf16[8,512,8,128]{1,3,2,0:T(8,128)(2,1)} fusion(bf16[8,8,128,512]{3,2,1,0:T(8,128)(2,1)} %bitcast.77, bf16[8,8,128,128]{3,2,1,0:T(8,128)(2,1)S(1)} %copy-done.2, pred[8]{0:T(512)(128)(4,1)S(1)} %compare_and_fusion.2), kind=kOutput, calls=%fused_computation.14 | convolution fusion | flops 1078984704 | bytes 18874376 | tf_op jit(solution)/shard_map/dtkr,dtkj->drtj/dot_general | solution.py:102
  373.5 12.7 %copy.95 = bf16[8,512,8,128]{3,2,1,0:T(8,128)(2,1)} copy(bf16[8,512,8,128]{1,3,2,0:T(8,128)(2,1)} %convert_bitcast_fusion) | data formatting | bytes 16777216 | tf_op jit(solution)/shard_map/convert_element_type | solution.py:104
  386.2 8.8 %copy.116 = bf16[512,8,8,128]{3,1,2,0:T(8,128)(2,1)} copy(bf16[512,8,8,128]{3,2,1,0:T(8,128)(2,1)} %bitcast.80) | data formatting | bytes 16777216
  396.2 9.9 %gather_fusion = bf16[1024,32,128]{2,1,0:T(8,128)(2,1)} fusion(bf16[32,128,128]{2,0,1:T(8,128)(2,1)S(1)} %copy.77, s32[1024]{0:T(1024)S(1)} %broadcast_clamp_fusion.1), kind=kCustom, calls=%fused_computation | custom fusion | bytes 16781312 | tf_op jit(solution)/shard_map/jit(_take)/gather | solution.py:66
  406.1 7.2 %convert_bitcast_fusion.2 = bf16[32,128,8,128]{3,2,0,1:T(8,128)(2,1)S(1)} fusion(bf16[128,8,32,128]{3,2,1,0:T(8,128)(2,1)} %bitcast.81, pred[128,8]{1,0:T(8,128)(4,1)S(1)} %copy.73, s32[128,8]{1,0:T(8,128)S(1)} %copy.72, s32[128,8]{1,0:T(8,128)S(1)} %copy.71), kind=kOutput, calls=%fused_computation.16 | convolution fusion | flops 75522048 | bytes 16786432 | tf_op jit(solution)/shard_map/cpki,pkg->cpgi/dot_general | solution.py:72
  413.3 6.1 %bitcast_convert_fusion = bf16[32,128,128]{2,1,0:T(8,128)(2,1)} fusion(bf16[32,128,8,128]{3,2,0,1:T(8,128)(2,1)S(1)} %convert_bitcast_fusion.2, bf16[8,128,128]{2,1,0:T(8,128)(2,1)S(1)} %copy-done.10), kind=kOutput, calls=%fused_computation.21 | convolution fusion | flops 1074266112 | bytes 9699328 | tf_op jit(solution)/shard_map/cpgj,gij->cpi/dot_general | solution.py:75
  419.4 1.7 convert_element_type.53
  421.7 34.0 %all_to_all.36 = bf16[32,32,512]{2,0,1:T(8,128)(2,1)S(1)} all-to-all(bf16[32,32,512]{2,0,1:T(8,128)(2,1)S(1)} %copy.80), channel_id=1, replica_groups=mesh['sym'=8,'rows'=32] {'rows'}, dimensions={1} | all-to-all | bytes 2097152 | tf_op jit(solution)/shard_map/all_to_all | solution.py:78
  455.8 1.6 transpose.48
  457.4 3.0 copy.81
  460.3 5.1 %fusion.12 = f32[512,1024]{1,0:T(8,128)} fusion(f32[1024,512]{0,1:T(8,128)} %copy.81, bf16[512,1024]{1,0:T(8,128)(2,1)} %reduce-scatter.2.cloned.1.call-done, bf16[512,1024]{1,0:T(8,128)(2,1)S(1)} %copy-done.3, bf16[1,1024,1024]{2,1,0:T(8,128)(2,1)} %param.12), kind=kOutput, calls=%fused_computation.20 | convolution fusion | flops 1075314688 | bytes 8388608 | tf_op jit(solution)/shard_map/dot_general | solution.py:62
  (54 shorter events, 5.1 us)
Async XLA Ops:
  6.5 249.1 %copy-start = (bf16[1,8,8,128,128]{4,3,2,1,0:T(8,128)(2,1)S(1)}, bf16[1,8,8,128,128]{4,3,2,1,0:T(8,128)(2,1)}, u32[]{:S(2)}) copy-start(bf16[1,8,8,128,128]{4,3,2,1,0:T(8,128)(2,1)} %param.13) | copy-start | bytes 6291460
  6.5 15.0 %copy-start.1 = (s32[32,32,2]{1,2,0:T(2,128)S(1)}, s32[32,32,2]{1,2,0:T(2,128)}, u32[]{:S(2)}) copy-start(s32[32,32,2]{1,2,0:T(2,128)} %param.15) | copy-start | bytes 24580
  9.0 39.7 %all-to-all-start = ((bf16[32,32,512]{2,1,0:T(8,128)(2,1)}), bf16[32,32,512]{2,1,0:T(8,128)(2,1)S(1)}, u32[]{:S(2)}, u32[]{:S(2)}) async-start(bf16[32,32,512]{2,1,0:T(8,128)(2,1)} %bitcast.84), calls=%async_computation | async-start | bytes 2097152 | tf_op jit(solution)/shard_map/all_to_all | solution.py:64
  21.5 20.3 %copy-start.4 = (s32[128,16]{0,1:T(8,128)S(1)}, s32[128,16]{0,1:T(8,128)}, u32[]{:S(2)}) copy-start(s32[128,16]{0,1:T(8,128)} %param.16) | copy-start | bytes 24580
  21.5 20.6 %copy-start.6 = (s32[128,16]{0,1:T(8,128)S(1)}, s32[128,16]{0,1:T(8,128)}, u32[]{:S(2)}) copy-start(s32[128,16]{0,1:T(8,128)} %param.18) | copy-start | bytes 24580
  21.5 20.7 %copy-start.7 = (s32[128,16]{0,1:T(8,128)S(1)}, s32[128,16]{0,1:T(8,128)}, u32[]{:S(2)}) copy-start(s32[128,16]{0,1:T(8,128)} %param.17) | copy-start | bytes 24580
  149.7 97.5 %all-to-all-start.2 = ((bf16[32,8,16,512]{3,2,1,0:T(8,128)(2,1)}), bf16[32,8,16,512]{3,2,1,0:T(8,128)(2,1)}, u32[]{:S(2)}, u32[]{:S(2)}) async-start(bf16[32,8,16,512]{3,2,1,0:T(8,128)(2,1)} %copy.91), calls=%async_computation.2 | async-start | bytes 8388608 | tf_op jit(solution)/shard_map/all_to_all | solution.py:38
  247.2 100.6 %all-to-all-start.3 = ((bf16[32,8,16,512]{3,2,1,0:T(8,128)(2,1)}), bf16[32,8,16,512]{3,2,1,0:T(8,128)(2,1)}, u32[]{:S(2)}, u32[]{:S(2)}) async-start(bf16[32,8,16,512]{3,2,1,0:T(8,128)(2,1)} %copy.92), calls=%async_computation.3 | async-start | bytes 8388608 | tf_op jit(solution)/shard_map/all_to_all | solution.py:38
  255.6 204.7 %reduce-scatter.2.cloned.1.call-start = ((), (), s32[]{:S(2)}) async-start(), calls=%async_computation.5 | async-start | bytes 9437184 | tf_op jit(solution)/shard_map/reduce_scatter | solution.py:103
  356.0 8.4 %copy-start.2 = (bf16[8,8,128,128]{3,2,1,0:T(8,128)(2,1)S(1)}, bf16[8,8,128,128]{3,2,1,0:T(8,128)(2,1)}, u32[]{:S(2)}) copy-start(bf16[8,8,128,128]{3,2,1,0:T(8,128)(2,1)} %gather_fusion.1) | copy-start | bytes 6291460
  395.0 0.7 copy-start.5
  395.0 0.9 copy-start.9
  395.0 1.0 copy-start.8
  406.1 7.2 %copy-start.10 = (bf16[8,128,128]{2,1,0:T(8,128)(2,1)S(1)}, bf16[8,128,128]{2,1,0:T(8,128)(2,1)}, u32[]{:S(2)}) copy-start(bf16[8,128,128]{2,1,0:T(8,128)(2,1)} %param.14) | copy-start | bytes 786436
  421.7 38.6 %copy-start.3 = (bf16[512,1024]{1,0:T(8,128)(2,1)S(1)}, bf16[512,1024]{1,0:T(8,128)(2,1)}, u32[]{:S(2)}) copy-start(bf16[512,1024]{1,0:T(8,128)(2,1)} %param.11) | copy-start | bytes 3145732
Sparse Core Ops, SparseCore 0:
  395.1 51.5 reduce-scatter.1
where the time goes:
time: 480 us; the launch traced here: 473 us
  waiting for transfers between devices  182 us (38%)
  local copies, waits for them, and re-layouts  139 us (29%)
  matrix products  53.3 us (11%)
  blocking collectives  34 us (7%)
  starting transfers between devices  25.7 us (5%)
  other arithmetic  25 us (5%)
  between operations  14 us (3%)
    all_to_all x2, waiting for transfers between devices, exchange_in_pieces(): lax.all_to_all(slab, axis, split_axis=0, concat_axis=0, tiled=True)  175 us
    all_to_all x1, blocking collectives, per_device(): lax.all_to_all(alpha_part.astype(jnp.bfloat16), 'rows', split_axis=1, con...  34 us
    dot_general x1, matrix products, per_device(): jnp.einsum('cpli,dpl->dcpi', gathered, mix_weight, preferred_element_type...  25.9 us
    gather x3, local copies, waits for them, and re-layouts, per_device(): owned_blk = send_list[slot_src, dest_rank, slot_pos]  20.2 us
    gather x1, local copies, waits for them, and re-layouts, per_device(): gathered = jnp.take(col_blocks, source, axis=1)  19.2 us
    split x3, local copies, waits for them, and re-layouts, exchange_in_pieces(): jnp.split(parts, piece_ends(parts.shape[widest], pieces), axis=widest)  16.1 us
    select_n x1, other arithmetic, per_device(): gathered = jnp.take(col_blocks, source, axis=1)  14.4 us
    all_to_all x2, starting transfers between devices, exchange_in_pieces(): lax.all_to_all(slab, axis, split_axis=0, concat_axis=0, tiled=True)  14 us
  transfers between devices with their start and end apart: 4, of which 3 were waited for; matrix products, arithmetic and copies ran while one was open for 13% of the time, Pallas kernels for 0%

commit v1 on v0

--- a/solution.py
+++ b/solution.py
@@ -8,6 +8,13 @@
 ABLK = 4
 CAP = 2
 NPA = 8
+
+
+def exchange_blocks(x, mesh_axis, split, join):
+    peers = lax.axis_size(mesh_axis)
+    shards = jnp.stack(jnp.split(x, peers, axis=split), axis=0)
+    shards = lax.all_to_all(shards, mesh_axis, split_axis=0, concat_axis=0)
+    return jnp.concatenate(shards, axis=join)
 
 
 def cut_along(array, dim, devices):
@@ -75,9 +82,9 @@
     alpha_part = jnp.einsum(
         "cpgj,gij->cpi", combined, pair_op, preferred_element_type=jnp.float32
     ).reshape(col_width, total_rows)
-    returned = lax.all_to_all(
-        alpha_part.astype(jnp.bfloat16), "rows", split_axis=1, concat_axis=0, tiled=True
-    ).astype(alpha_part.dtype)
+    returned = exchange_blocks(alpha_part.astype(jnp.bfloat16), "rows", 1, 0).astype(
+        alpha_part.dtype
+    )
     dest_ids = jnp.arange(sectors, dtype=jnp.int32)
     pair_of = jnp.bitwise_xor(sector, dest_ids)
     operators = jnp.take(mix_op[0], pair_of, axis=0)

time: 480 us -> 478 us (level)
    unnamed x26 -> x58, local copies, waits for them, and re-layouts: 12.1 us -> 12.9 us
  transfers between devices with their start and end apart: 4 -> 4, of which waited for: 3 -> 3; matrix products, arithmetic and copies ran while one was open for 13% -> 12% of each run, Pallas kernels for 0% -> 0%
where the time goes in v1:
time: 478 us; the launch traced here: 470 us
  waiting for transfers between devices  182 us (38%)
  local copies, waits for them, and re-layouts  138 us (29%)
  matrix products  52.3 us (11%)
  blocking collectives  33.9 us (7%)
  starting transfers between devices  25.7 us (5%)
  other arithmetic  25.1 us (5%)
  between operations  14.3 us (3%)
    all_to_all x2, waiting for transfers between devices, exchange_in_pieces(): lax.all_to_all(slab, axis, split_axis=0, concat_axis=0, tiled=True)  175 us
    all_to_all x1, blocking collectives, exchange_blocks(): shards = lax.all_to_all(shards, mesh_axis, split_axis=0, concat_axis=0)  33.9 us
    dot_general x1, matrix products, per_device(): jnp.einsum('cpli,dpl->dcpi', gathered, mix_weight, preferred_element_type...  25.9 us
    gather x3, local copies, waits for them, and re-layouts, per_device(): owned_blk = send_list[slot_src, dest_rank, slot_pos]  20.2 us
    gather x1, local copies, waits for them, and re-layouts, per_device(): gathered = jnp.take(col_blocks, source, axis=1)  19.2 us
    split x3, local copies, waits for them, and re-layouts, exchange_in_pieces(): jnp.split(parts, piece_ends(parts.shape[widest], pieces), axis=widest)  16.1 us
    select_n x1, other arithmetic, per_device(): gathered = jnp.take(col_blocks, source, axis=1)  14.4 us
    all_to_all x2, starting transfers between devices, exchange_in_pieces(): lax.all_to_all(slab, axis, split_axis=0, concat_axis=0, tiled=True)  14 us
  transfers between devices with their start and end apart: 4, of which 3 were waited for; matrix products, arithmetic and copies ran while one was open for 12% of the time, Pallas kernels for 0%

profile of v1, /device:TPU:18, one launch (start us, length us, event | category | flops | bytes accessed | tf_op | source)
XLA Modules:
  0.0 470.4 jit_solution(17785702080116994374)
XLA Ops:
  6.5 2.4 copy.103
  9.0 11.6 %all-to-all-start = ((bf16[32,32,512]{2,1,0:T(8,128)(2,1)}), bf16[32,32,512]{2,1,0:T(8,128)(2,1)S(1)}, u32[]{:S(2)}, u32[]{:S(2)}) async-start(bf16[32,32,512]{2,1,0:T(8,128)(2,1)} %bitcast.247), calls=%async_computation | async-start | bytes 2097152 | tf_op jit(solution)/shard_map/all_to_all | solution.py:71
  21.5 20.1 %gather_fusion.2 = s32[2048]{0:T(1024)S(1)} fusion(s32[32,32,2]{1,2,0:T(2,128)S(1)} %copy-done.1, s32[2048]{0:T(1024)S(1)} %reshape.93), kind=kCustom, calls=%fused_computation.2 | custom fusion | bytes 40960 | tf_op jit(solution)/shard_map/gather | solution.py:95
  42.4 6.2 %all-to-all-done = bf16[32,32,512]{2,1,0:T(8,128)(2,1)S(1)} async-done(((bf16[32,32,512]{2,1,0:T(8,128)(2,1)}), bf16[32,32,512]{2,1,0:T(8,128)(2,1)S(1)}, u32[]{:S(2)}, u32[]{:S(2)}) %all-to-all-start) | async-done | bytes 1048608 | tf_op jit(solution)/shard_map/all_to_all | solution.py:71
  48.7 1.5 copy.104
  50.2 2.5 reshape.75
  52.7 1.9 copy.106
  54.6 19.2 %gather_fusion.3 = bf16[2048,32,128]{2,1,0:T(8,128)(2,1)} fusion(bf16[32,128,128]{2,0,1:T(8,128)(2,1)S(1)} %copy.106, s32[2048]{0:T(1024)S(1)} %broadcast_clamp_fusion), kind=kCustom, calls=%fused_computation.3 | custom fusion | bytes 33562624 | tf_op jit(solution)/shard_map/jit(_take)/gather | solution.py:97
  73.8 14.4 %select_bitcast_fusion = bf16[32,128,16,128]{3,0,2,1:T(8,128)(2,1)} fusion(bf16[128,16,32,128]{3,2,1,0:T(8,128)(2,1)} %bitcast.208, pred[128,16]{1,0:T(8,128)(4,1)S(1)} %copy.114), kind=kLoop, calls=%fused_computation.6 | loop fusion | flops 8388608 | bytes 33556480 | tf_op jit(solution)/shard_map/jit(_take)/select_n | solution.py:97
  88.2 25.9 %convert_bitcast_fusion.1 = bf16[8,32,128,128]{3,0,1,2:T(8,128)(2,1)} fusion(bf16[32,128,16,128]{3,0,2,1:T(8,128)(2,1)} %select_bitcast_fusion, bf16[128,16]{1,0:T(8,128)(2,1)S(1)} %copy.111, s32[128,16]{1,0:T(8,128)S(1)} %copy.110, s32[8]{0:T(128)S(1)} %iota_xor_fusion), kind=kOutput, calls=%fused_computation.15 | convolution fusion | flops 138444800 | bytes 25178144 | tf_op jit(solution)/shard_map/cpli,dpl->dcpi/dot_general | solution.py:101
  114.1 12.0 %copy.118 = bf16[8,32,128,128]{3,2,1,0:T(8,128)(2,1)} copy(bf16[8,32,128,128]{3,0,1,2:T(8,128)(2,1)} %convert_bitcast_fusion.1) | data formatting | bytes 16777216 | tf_op jit(solution)/shard_map/convert_element_type | solution.py:103
  126.1 14.0 %reshape_reshape.6 = bf16[8,32,32,512]{3,2,1,0:T(8,128)(2,1)} reshape(bf16[8,32,128,128]{3,2,1,0:T(8,128)(2,1)} %copy.118) | data formatting | bytes 16777216 | tf_op jit(solution)/shard_map/reshape;reshape | solution.py:22
  140.1 5.3 %fusion.51 = (bf16[32,8,16,512]{3,0,2,1:T(8,128)(2,1)S(1)}, bf16[32,8,16,512]{3,0,2,1:T(8,128)(2,1)}) fusion(bf16[32,8,32,512]{3,0,2,1:T(8,128)(2,1)} %bitcast.211), kind=kLoop, calls=%fused_computation.149 | loop fusion | bytes 16777216 | tf_op jit(solution)/shard_map/split | solution.py:43
  145.4 4.3 copy.119
  149.7 5.6 %all-to-all-start.2 = ((bf16[32,8,16,512]{3,2,1,0:T(8,128)(2,1)}), bf16[32,8,16,512]{3,2,1,0:T(8,128)(2,1)}, u32[]{:S(2)}, u32[]{:S(2)}) async-start(bf16[32,8,16,512]{3,2,1,0:T(8,128)(2,1)} %copy.119), calls=%async_computation.2 | async-start | bytes 8388608 | tf_op jit(solution)/shard_map/all_to_all | solution.py:45
  155.3 6.5 %copy.120 = bf16[32,8,16,512]{3,2,1,0:T(8,128)(2,1)} copy(bf16[32,8,16,512]{3,0,2,1:T(8,128)(2,1)} %get-tuple-element.8) | data formatting | bytes 8388608 | tf_op jit(solution)/shard_map/split | solution.py:43
  161.8 85.3 %all-to-all-done.2 = bf16[32,8,16,512]{3,2,1,0:T(8,128)(2,1)} async-done(((bf16[32,8,16,512]{3,2,1,0:T(8,128)(2,1)}), bf16[32,8,16,512]{3,2,1,0:T(8,128)(2,1)}, u32[]{:S(2)}, u32[]{:S(2)}) %all-to-all-start.2) | async-done | bytes 4194336 | tf_op jit(solution)/shard_map/all_to_all | solution.py:45
  247.2 8.4 %all-to-all-start.3 = ((bf16[32,8,16,512]{3,2,1,0:T(8,128)(2,1)}), bf16[32,8,16,512]{3,2,1,0:T(8,128)(2,1)}, u32[]{:S(2)}, u32[]{:S(2)}) async-start(bf16[32,8,16,512]{3,2,1,0:T(8,128)(2,1)} %copy.120), calls=%async_computation.3 | async-start | bytes 8388608 | tf_op jit(solution)/shard_map/all_to_all | solution.py:45
  255.7 2.1 gather_fusion.1
  257.8 90.0 %all-to-all-done.3 = bf16[32,8,16,512]{3,2,1,0:T(8,128)(2,1)} async-done(((bf16[32,8,16,512]{3,2,1,0:T(8,128)(2,1)}), bf16[32,8,16,512]{3,2,1,0:T(8,128)(2,1)}, u32[]{:S(2)}, u32[]{:S(2)}) %all-to-all-start.3) | async-done | bytes 4194336 | tf_op jit(solution)/shard_map/all_to_all | solution.py:45
  347.8 8.2 %maximum_bitcast_fusion = bf16[8,32,32,512]{3,2,0,1:T(8,128)(2,1)} fusion(bf16[32,8,16,512]{3,2,1,0:T(8,128)(2,1)} %all-to-all-done.3, bf16[32,8,16,512]{3,2,1,0:T(8,128)(2,1)} %all-to-all-done.2), kind=kLoop, calls=%fused_computation.8 | loop fusion | flops 16777216 | bytes 16777216 | tf_op jit(solution)/shard_map/transpose | solution.py:36
  356.0 8.4 %copy.121 = bf16[8,32,32,512]{3,2,1,0:T(8,128)(2,1)} copy(bf16[8,32,32,512]{3,2,0,1:T(8,128)(2,1)} %maximum_bitcast_fusion) | data formatting | bytes 16777216 | tf_op jit(solution)/shard_map/transpose | solution.py:36
  364.5 9.1 %convert_bitcast_fusion = bf16[8,512,8,128]{1,3,2,0:T(8,128)(2,1)} fusion(bf16[8,8,128,512]{3,2,1,0:T(8,128)(2,1)} %bitcast.209, bf16[8,8,128,128]{3,2,1,0:T(8,128)(2,1)S(1)} %copy-done.2, pred[8]{0:T(512)(128)(4,1)S(1)} %compare_and_fusion.2), kind=kOutput, calls=%fused_computation.14 | convolution fusion | flops 1078984704 | bytes 18874376 | tf_op jit(solution)/shard_map/dtkr,dtkj->drtj/dot_general | solution.py:109
  373.5 12.7 %copy.123 = bf16[8,512,8,128]{3,2,1,0:T(8,128)(2,1)} copy(bf16[8,512,8,128]{1,3,2,0:T(8,128)(2,1)} %convert_bitcast_fusion) | data formatting | bytes 16777216 | tf_op jit(solution)/shard_map/convert_element_type | solution.py:111
  386.2 8.8 %copy.146 = bf16[512,8,8,128]{3,1,2,0:T(8,128)(2,1)} copy(bf16[512,8,8,128]{3,2,1,0:T(8,128)(2,1)} %bitcast.212) | data formatting | bytes 16777216
  396.2 9.9 %gather_fusion = bf16[1024,32,128]{2,1,0:T(8,128)(2,1)} fusion(bf16[32,128,128]{2,0,1:T(8,128)(2,1)S(1)} %copy.106, s32[1024]{0:T(1024)S(1)} %broadcast_clamp_fusion.1), kind=kCustom, calls=%fused_computation | custom fusion | bytes 16781312 | tf_op jit(solution)/shard_map/jit(_take)/gather | solution.py:73
  406.1 7.2 %convert_bitcast_fusion.2 = bf16[32,128,8,128]{3,2,0,1:T(8,128)(2,1)S(1)} fusion(bf16[128,8,32,128]{3,2,1,0:T(8,128)(2,1)} %bitcast.213, pred[128,8]{1,0:T(8,128)(4,1)S(1)} %copy.102, s32[128,8]{1,0:T(8,128)S(1)} %copy.101, s32[128,8]{1,0:T(8,128)S(1)} %copy.100), kind=kOutput, calls=%fused_computation.16 | convolution fusion | flops 75522048 | bytes 16786432 | tf_op jit(solution)/shard_map/cpki,pkg->cpgi/dot_general | solution.py:79
  413.3 5.1 %bitcast_convert_fusion = bf16[32,128,128]{2,1,0:T(8,128)(2,1)S(1)} fusion(bf16[32,128,8,128]{3,2,0,1:T(8,128)(2,1)S(1)} %convert_bitcast_fusion.2, bf16[8,128,128]{2,1,0:T(8,128)(2,1)S(1)} %copy-done.10), kind=kOutput, calls=%fused_computation.21 | convolution fusion | flops 1074266112 | bytes 9699328 | tf_op jit(solution)/shard_map/cpgj,gij->cpi/dot_general | solution.py:82
  419.5 33.9 %all_to_all.31 = bf16[32,32,512]{2,1,0:T(8,128)(2,1)S(1)} all-to-all(bf16[32,32,512]{2,1,0:T(8,128)(2,1)S(1)} %constant_dynamic-update-slice_fusion), channel_id=1, replica_groups=mesh['sym'=8,'rows'=32] {'rows'}, dimensions={0} | all-to-all | bytes 2097152 | tf_op jit(solution)/shard_map/all_to_all | solution.py:16
  453.4 1.7 bitcast_convert_fusion.1
  455.1 3.0 copy.109
  458.1 5.1 %fusion.12 = f32[512,1024]{1,0:T(8,128)} fusion(f32[1024,512]{0,1:T(8,128)} %copy.109, bf16[512,1024]{1,0:T(8,128)(2,1)} %reduce-scatter.2.cloned.1.call-done, bf16[512,1024]{1,0:T(8,128)(2,1)S(1)} %copy-done.3, bf16[1,1024,1024]{2,1,0:T(8,128)(2,1)} %param.12), kind=kOutput, calls=%fused_computation.20 | convolution fusion | flops 1075314688 | bytes 8388608 | tf_op jit(solution)/shard_map/dot_general | solution.py:69
  (85 shorter events, 3.8 us)
Async XLA Ops:
  6.5 249.1 %copy-start = (bf16[1,8,8,128,128]{4,3,2,1,0:T(8,128)(2,1)S(1)}, bf16[1,8,8,128,128]{4,3,2,1,0:T(8,128)(2,1)}, u32[]{:S(2)}) copy-start(bf16[1,8,8,128,128]{4,3,2,1,0:T(8,128)(2,1)} %param.13) | copy-start | bytes 6291460
  6.5 15.0 %copy-start.1 = (s32[32,32,2]{1,2,0:T(2,128)S(1)}, s32[32,32,2]{1,2,0:T(2,128)}, u32[]{:S(2)}) copy-start(s32[32,32,2]{1,2,0:T(2,128)} %param.15) | copy-start | bytes 24580
  9.0 39.7 %all-to-all-start = ((bf16[32,32,512]{2,1,0:T(8,128)(2,1)}), bf16[32,32,512]{2,1,0:T(8,128)(2,1)S(1)}, u32[]{:S(2)}, u32[]{:S(2)}) async-start(bf16[32,32,512]{2,1,0:T(8,128)(2,1)} %bitcast.247), calls=%async_computation | async-start | bytes 2097152 | tf_op jit(solution)/shard_map/all_to_all | solution.py:71
  21.5 20.3 %copy-start.4 = (s32[128,16]{0,1:T(8,128)S(1)}, s32[128,16]{0,1:T(8,128)}, u32[]{:S(2)}) copy-start(s32[128,16]{0,1:T(8,128)} %param.16) | copy-start | bytes 24580
  21.5 20.6 %copy-start.6 = (s32[128,16]{0,1:T(8,128)S(1)}, s32[128,16]{0,1:T(8,128)}, u32[]{:S(2)}) copy-start(s32[128,16]{0,1:T(8,128)} %param.18) | copy-start | bytes 24580
  21.5 20.7 %copy-start.7 = (s32[128,16]{0,1:T(8,128)S(1)}, s32[128,16]{0,1:T(8,128)}, u32[]{:S(2)}) copy-start(s32[128,16]{0,1:T(8,128)} %param.17) | copy-start | bytes 24580
  149.7 97.5 %all-to-all-start.2 = ((bf16[32,8,16,512]{3,2,1,0:T(8,128)(2,1)}), bf16[32,8,16,512]{3,2,1,0:T(8,128)(2,1)}, u32[]{:S(2)}, u32[]{:S(2)}) async-start(bf16[32,8,16,512]{3,2,1,0:T(8,128)(2,1)} %copy.119), calls=%async_computation.2 | async-start | bytes 8388608 | tf_op jit(solution)/shard_map/all_to_all | solution.py:45
  247.2 100.6 %all-to-all-start.3 = ((bf16[32,8,16,512]{3,2,1,0:T(8,128)(2,1)}), bf16[32,8,16,512]{3,2,1,0:T(8,128)(2,1)}, u32[]{:S(2)}, u32[]{:S(2)}) async-start(bf16[32,8,16,512]{3,2,1,0:T(8,128)(2,1)} %copy.120), calls=%async_computation.3 | async-start | bytes 8388608 | tf_op jit(solution)/shard_map/all_to_all | solution.py:45
  255.6 202.5 %reduce-scatter.2.cloned.1.call-start = ((), (), s32[]{:S(2)}) async-start(), calls=%async_computation.5 | async-start | bytes 9437184 | tf_op jit(solution)/shard_map/reduce_scatter | solution.py:110
  356.0 8.4 %copy-start.2 = (bf16[8,8,128,128]{3,2,1,0:T(8,128)(2,1)S(1)}, bf16[8,8,128,128]{3,2,1,0:T(8,128)(2,1)}, u32[]{:S(2)}) copy-start(bf16[8,8,128,128]{3,2,1,0:T(8,128)(2,1)} %gather_fusion.1) | copy-start | bytes 6291460
  395.0 0.7 copy-start.5
  395.0 0.9 copy-start.9
  395.0 1.0 copy-start.8
  406.1 7.2 %copy-start.10 = (bf16[8,128,128]{2,1,0:T(8,128)(2,1)S(1)}, bf16[8,128,128]{2,1,0:T(8,128)(2,1)}, u32[]{:S(2)}) copy-start(bf16[8,128,128]{2,1,0:T(8,128)(2,1)} %param.14) | copy-start | bytes 786436
  418.4 39.6 %copy-start.3 = (bf16[512,1024]{1,0:T(8,128)(2,1)S(1)}, bf16[512,1024]{1,0:T(8,128)(2,1)}, u32[]{:S(2)}) copy-start(bf16[512,1024]{1,0:T(8,128)(2,1)} %param.11) | copy-start | bytes 3145732
Sparse Core Ops, SparseCore 0:
  395.1 51.5 reduce-scatter.1
